TPU v7x, 256 devices: a whole 4x4x8 slice. The times are simulated.
256 devices in a mesh: grp: 8 (over z_hi, y), sp: 32 (over z_lo, x, core).
Axes of the slice: x: 4, y: 4, z: 8 (z_hi: 2, z_lo: 4; z = z_hi * 4 + z_lo), core: 2. Of those that a mesh axis runs over, the one named last changes fastest.
Arguments:
- alpha: float32 [80, 32, 4096], P('grp', None, 'sp'), may hold values from -6 to 6
- ensemble: bfloat16 [80, 3, 32, 4096], P('grp', None, None, 'sp'), may hold values from -6 to 6
- static_std: float32 [3, 32, 4096], P(None, 'grp', 'sp'), may hold values from 0.2 to 1
- control: float32 [3, 32, 4096], P(None, 'grp', 'sp'), may hold values from -6 to 6
- loc_spectrum: float32 [1024], replicated, may hold values from 0.00024414062 to 0.001953125
- obs_cell: int32 [262144], P(('grp', 'sp')), may hold values from 0 to 131071, as said below
- obs_step: int32 [262144], P(('grp', 'sp')), may hold values from 0 to 2
- innovation: float32 [262144], P(('grp', 'sp')), may hold values from -6 to 6
- obs_weight: float32 [262144], P(('grp', 'sp')), may hold values from 0.5 to 4
Outputs:
- grad_alpha: float32 [80, 32, 4096], P('grp', None, 'sp')
- grad_control: float32 [3, 32, 4096], P(None, 'grp', 'sp')
Inputs may be any that keep to these rules, and one draw needn't show every extreme that they name: `obs_cell`: an entry is row * 4096 + column. Entries 1024 * b to 1024 * (b + 1) - 1 lie in the tile of 4 rows from row 4 * (b // 32) and 128 columns from column 128 * (b % 32).
All inputs are finite; a program needn't handle non-finite values.
Results may differ from a plain program's by a relative error of at most 0.0075.
Values may be sent and summed in bfloat16 or wider, within the bound.
No kernel may reach another device: no remote copies, remote signals or barrier semaphores. Data moves between devices by JAX's collectives and lax.ppermute only.
A program may use at most 128 MiB of HBM per device.

v0:
```python
import math
import jax
import jax.numpy as jnp
from jax import lax
from jax.sharding import Mesh
from jax.sharding import PartitionSpec as P

NX = 4096
GRP_SP = ("grp", "sp_0", "sp_1", "sp_2")
SP = ("sp_0", "sp_1", "sp_2")
courant = 0.4


def extended(block, sides, width):
    for axis, dim in sides:
        count = lax.axis_size(axis)
        forward = [(i, i + 1) for i in range(count - 1)]
        forward.append((count - 1, 0))
        backward = [(target, source) for source, target in forward]
        low = lax.ppermute(
            lax.slice_in_dim(block, block.shape[dim] - width, None, axis=dim), axis, forward
        )
        high = lax.ppermute(lax.slice_in_dim(block, 0, width, axis=dim), axis, backward)
        block = jnp.concatenate([low, block, high], axis=dim)
    return block


def in_blocks(x, dim, length):
    shape = x.shape
    tiles = x.reshape(*shape[:dim], length, shape[dim] // length, *shape[dim + 1 :])
    return jnp.moveaxis(tiles, dim, 0)


def sum_at_owner(x, axis, dim):
    tiles = in_blocks(x, dim, lax.axis_size(axis))
    arrived = lax.all_to_all(tiles, axis, split_axis=0, concat_axis=0, tiled=True)
    return arrived.sum(axis=0)


def in_order(tiles, dim):
    tiles = jnp.moveaxis(tiles, 0, dim)
    shape = tiles.shape
    return tiles.reshape(*shape[:dim], shape[dim] * shape[dim + 1], *shape[dim + 2 :])


def copy_for_each(x, axis):
    copies = jnp.broadcast_to(x, (lax.axis_size(axis), *x.shape))
    return lax.all_to_all(copies, axis, split_axis=0, concat_axis=0, tiled=True)


def gathered_copies(x, axis, dim):
    return in_order(copy_for_each(x, axis), dim)


def moved_by_axis(tiles, axes, turns):
    shape = [lax.axis_size(a) for a in axes]
    tiles = tiles.reshape(*shape, *tiles.shape[1:])
    for k in turns:
        tiles = lax.all_to_all(tiles, axes[k], split_axis=k, concat_axis=k, tiled=True)
    return tiles.reshape(-1, *tiles.shape[len(axes) :])


def core_and_chips(x, groups, turns, split_dim, concat_dim):
    length = lax.axis_size(groups[0]) * lax.axis_size(groups[1])
    tiles = in_blocks(x, split_dim, length)
    return in_order(moved_by_axis(tiles, groups, turns), concat_dim)


def spectral_filter(rows_data, loc_spectrum):
    length_x = rows_data.shape[1]
    kept_waves = loc_spectrum.shape[0]
    freq_block = math.gcd(kept_waves, 256)
    positions = jnp.arange(length_x, dtype=jnp.int32)
    filtered = jnp.zeros(rows_data.shape, jnp.float32)
    for start_wave in range(0, kept_waves, freq_block):
        waves = start_wave + jnp.arange(freq_block, dtype=jnp.int32)
        phases = positions[:, None] * waves[None, :] % length_x
        radians = 2.0 * math.pi / length_x * phases.astype(jnp.float32)
        fourier_basis = jnp.concatenate([jnp.cos(radians), jnp.sin(radians)], axis=1)
        weights = loc_spectrum[start_wave : start_wave + freq_block]
        weights = jnp.concatenate([weights, weights])
        coeffs = jnp.dot(
            rows_data,
            fourier_basis,
            precision=lax.Precision.HIGHEST,
            preferred_element_type=jnp.float32,
        )
        filtered = filtered + jnp.dot(
            coeffs * weights[None, :],
            fourier_basis.T,
            precision=lax.Precision.HIGHEST,
            preferred_element_type=jnp.float32,
        )
    return filtered


def inner(field):
    return field[..., 1:-1, 1:-1]


def diff_x(field):
    return 0.5 * (field[..., 1:-1, 2:] - field[..., 1:-1, :-2])


def diff_y(field):
    return 0.5 * (field[..., 2:, 1:-1] - field[..., :-2, 1:-1])


def clip_rows(stack, margin, first_row, total_rows):
    rows_index = first_row - margin + jnp.arange(stack.shape[1], dtype=jnp.int32)
    valid = jnp.logical_and(rows_index >= 0, rows_index < total_rows).astype(jnp.float32)
    return stack * valid[None, :, None]


def coriolis_rows(first_row, margin, count, total_rows):
    rows_index = first_row - margin + jnp.arange(count, dtype=jnp.int32)
    return (0.1 + 0.2 * (rows_index.astype(jnp.float32) + 0.5) / total_rows)[:, None]


def forward_a(stack, margin, first_row, total_rows):
    height, eastward, northward = (stack[0], stack[1], stack[2])
    new_height = inner(height) - courant * (diff_x(eastward) + diff_y(northward))
    result = jnp.stack([new_height, inner(eastward), inner(northward)])
    return clip_rows(result, margin - 1, first_row, total_rows)


def forward_b(stack, margin, first_row, total_rows):
    height, eastward, northward = (stack[0], stack[1], stack[2])
    rotation = coriolis_rows(first_row, margin - 1, stack.shape[1] - 2, total_rows)
    new_east = inner(eastward) - courant * diff_x(height) + rotation * inner(northward)
    new_north = inner(northward) - courant * diff_y(height) - rotation * inner(eastward)
    result = jnp.stack([inner(height), new_east, new_north])
    return clip_rows(result, margin - 1, first_row, total_rows)


def backward_a(stack, margin, first_row, total_rows):
    back_h, back_u, back_w = (stack[0], stack[1], stack[2])
    adj_height = inner(back_h) + courant * (diff_x(back_u) + diff_y(back_w))
    result = jnp.stack([adj_height, inner(back_u), inner(back_w)])
    return clip_rows(result, margin - 1, first_row, total_rows)


def backward_b(stack, margin, first_row, total_rows):
    adj_height, back_u, back_w = (stack[0], stack[1], stack[2])
    rotation = coriolis_rows(first_row, margin - 1, stack.shape[1] - 2, total_rows)
    adj_east = inner(back_u) - rotation * inner(back_w) + courant * diff_x(adj_height)
    adj_north = inner(back_w) + rotation * inner(back_u) + courant * diff_y(adj_height)
    result = jnp.stack([inner(adj_height), adj_east, adj_north])
    return clip_rows(result, margin - 1, first_row, total_rows)


def deep_rim(stack):
    return extended(stack, (("grp", 1), (SP, 2)), 4)


def per_device(
    alpha, ensemble, static_std, control, loc_spectrum, obs_cell, obs_step, innovation, obs_weight
):
    members_local = alpha.shape[0]
    groups = lax.axis_size("grp")
    spread = 1.0 / math.sqrt(members_local * groups - 1)
    tile_rows, tile_cols = (control.shape[1], control.shape[2])
    total_rows = tile_rows * groups
    first_row = lax.axis_index("grp") * tile_rows
    first_col = lax.axis_index(SP) * tile_cols

    def localize_items(items):
        dims = items.shape
        flat = items.reshape(dims[0] * dims[1], dims[2])
        return spectral_filter(flat, loc_spectrum).reshape(dims)

    def to_rows(columns):
        return localize_items(lax.all_to_all(columns, SP, split_axis=1, concat_axis=2, tiled=True))

    localized = lax.all_to_all(
        to_rows(alpha).astype(jnp.bfloat16), SP, split_axis=2, concat_axis=1, tiled=True
    )
    partial_value = jnp.einsum(
        "mvyx,myx->vyx", ensemble, localized, preferred_element_type=jnp.float32
    )
    summed = sum_at_owner(partial_value, "grp", 1)
    increment = static_std * control + spread * summed
    padded = clip_rows(deep_rim(increment), 4, first_row, total_rows)
    middle = forward_b(forward_a(padded, 4, first_row, total_rows), 3, first_row, total_rows)
    first_state = middle[:, 2:-2, 2:-2]
    second_state = forward_b(forward_a(middle, 2, first_row, total_rows), 1, first_row, total_rows)
    states = (increment, first_state, second_state)
    local_index = (obs_cell // NX - first_row) * tile_cols + (obs_cell % NX - first_col)
    observed = jnp.zeros(innovation.shape, jnp.float32)
    for moment in range(3):
        values = states[moment][0].reshape(-1)[local_index]
        observed = jnp.where(obs_step == moment, values, observed)
    misfit = obs_weight * (observed - innovation)
    forcings = []
    for moment in range(3):
        spread_obs = jnp.where(obs_step == moment, misfit, jnp.zeros_like(misfit))
        height_force = (
            jnp.zeros((tile_rows * tile_cols,), jnp.float32).at[local_index].add(spread_obs)
        )
        forcings.append(height_force.reshape(tile_rows, tile_cols))
    zero_field = jnp.zeros((tile_rows, tile_cols), jnp.float32)
    last_adjoint = jnp.stack([forcings[2], zero_field, zero_field])
    padded = clip_rows(
        deep_rim(jnp.concatenate([last_adjoint, forcings[1][None]], axis=0)),
        4,
        first_row,
        total_rows,
    )
    middle = backward_b(backward_a(padded[:3], 4, first_row, total_rows), 3, first_row, total_rows)
    middle = middle.at[0].add(padded[3, 2:-2, 2:-2])
    adjoint = backward_b(backward_a(middle, 2, first_row, total_rows), 1, first_row, total_rows)
    adjoint = adjoint.at[0].add(forcings[0])
    grad_control = control + static_std * adjoint
    half = adjoint.astype(jnp.bfloat16)
    weighted = jnp.einsum(
        "mvyx,vyx->myx",
        ensemble,
        gathered_copies(half, "grp", 1),
        preferred_element_type=jnp.float32,
    )
    filtered = core_and_chips(to_rows(weighted), (("sp_0", "sp_1"), "sp_2"), (1, 0), 2, 1)
    grad_alpha = alpha + spread * filtered
    return (grad_alpha, grad_control)


def solution(mesh):
    torus = Mesh(mesh.devices.reshape(mesh.shape["grp"], 4, 4, 2), ("grp", "sp_0", "sp_1", "sp_2"))
    placed = (
        P("grp", None, SP),
        P("grp", None, None, SP),
        P(None, "grp", SP),
        P(None, "grp", SP),
        P(),
        P(GRP_SP),
        P(GRP_SP),
        P(GRP_SP),
        P(GRP_SP),
    )
    return jax.shard_map(
        per_device,
        mesh=torus,
        in_specs=placed,
        out_specs=(P("grp", None, SP), P(None, "grp", SP)),
        check_vma=False,
    )
```

profile of v0, /device:TPU:1, one launch (start us, length us, event | category | flops | bytes accessed | tf_op | source)
XLA Modules:
  0.0 377.0 jit_solution(4057525190884514991)
XLA Ops:
  2.4 10.0 %all-to-all-start = ((f32[10,32,128]{2,0,1:T(8,128)}), f32[10,32,128]{2,0,1:T(8,128)S(1)}, u32[]{:S(2)}, u32[]{:S(2)}) async-start(f32[10,32,128]{2,0,1:T(8,128)} %copy.25), calls=%async_computation | async-start | bytes 524288 | tf_op jit(solution)/shard_map/all_to_all | solution.py:173
  12.4 17.6 %fusion.36 = (f32[4096,256]{1,0:T(8,128)}, f32[4096,256]{1,0:T(8,128)}) fusion(), kind=kLoop, calls=%fused_computation.64 | loop fusion | flops 14680064 | bytes 8388608 | tf_op jit(solution)/shard_map/sin | solution.py:79
  30.1 17.9 %fusion.43 = (f32[4096,256]{1,0:T(8,128)}, f32[4096,256]{1,0:T(8,128)}) fusion(s32[256]{0:T(256)S(1)} %iota_add_fusion.2), kind=kLoop, calls=%fused_computation.71 | loop fusion | flops 14680064 | bytes 8389632 | tf_op jit(solution)/shard_map/cos | solution.py:79
  47.9 17.9 %fusion.41 = (f32[4096,256]{1,0:T(8,128)}, f32[4096,256]{1,0:T(8,128)}) fusion(s32[256]{0:T(256)S(1)} %iota_add_fusion.1), kind=kLoop, calls=%fused_computation.69 | loop fusion | flops 14680064 | bytes 8389632 | tf_op jit(solution)/shard_map/cos | solution.py:79
  65.8 17.9 %fusion.39 = (f32[4096,256]{1,0:T(8,128)}, f32[4096,256]{1,0:T(8,128)}) fusion(s32[256]{0:T(256)S(1)} %iota_add_fusion), kind=kLoop, calls=%fused_computation.67 | loop fusion | flops 14680064 | bytes 8389632 | tf_op jit(solution)/shard_map/cos | solution.py:79
  84.1 7.5 %fusion.44 = f32[512,10]{0,1:T(8,128)S(1)} fusion(f32[10,4096]{1,0:T(8,128)S(1)} %bitcast.186, f32[4096,256]{1,0:T(8,128)} %get-tuple-element.102, f32[4096,256]{1,0:T(8,128)} %get-tuple-element.103, f32[512]{0:T(512)S(1)} %get-tuple-element.98), kind=kOutput, calls=%fused_computation.72 | convolution fusion | flops 253760512 | bytes 8574976 | tf_op jit(solution)/shard_map/dot_general | solution.py:82
  91.6 7.0 %fusion.34 = f32[10,4096]{1,0:T(8,128)S(1)} fusion(f32[512,10]{0,1:T(8,128)S(1)} %fusion.44, f32[4096,256]{1,0:T(8,128)S(1)} %copy-done, f32[4096,256]{1,0:T(8,128)S(1)} %copy-done.2), kind=kOutput, calls=%fused_computation.62 | convolution fusion | flops 253755392 | bytes 8572928 | tf_op jit(solution)/shard_map/dot_general | solution.py:88
  103.1 7.2 %convolution_add_fusion.5 = f32[10,4096]{1,0:T(8,128)S(1)} fusion(f32[10,4096]{1,0:T(8,128)S(1)} %fusion.34, f32[512,10]{0,1:T(8,128)S(1)} %fusion.46, f32[4096,256]{1,0:T(8,128)S(1)} %copy-done.14, f32[4096,256]{1,0:T(8,128)S(1)} %copy-done.12), kind=kOutput, calls=%fused_computation.27 | convolution fusion | flops 253796352 | bytes 8736768 | tf_op jit(solution)/shard_map/dot_general | solution.py:88
  114.9 7.2 %convolution_add_fusion.4 = f32[10,4096]{1,0:T(8,128)S(1)} fusion(f32[10,4096]{1,0:T(8,128)S(1)} %convolution_add_fusion.5, f32[512,10]{0,1:T(8,128)S(1)} %fusion.48, f32[4096,256]{1,0:T(8,128)S(1)} %copy-done.10, f32[4096,256]{1,0:T(8,128)S(1)} %copy-done.8), kind=kOutput, calls=%fused_computation.26 | convolution fusion | flops 253796352 | bytes 8736768 | tf_op jit(solution)/shard_map/dot_general | solution.py:88
  126.6 7.4 %fusion.1 = bf16[10,1,4096]{2,0,1:T(8,128)(2,1)S(1)} fusion(f32[10,4096]{1,0:T(8,128)S(1)} %convolution_add_fusion.4, f32[512,10]{0,1:T(8,128)S(1)} %fusion.50, f32[4096,256]{1,0:T(8,128)S(1)} %copy-done.6, f32[4096,256]{1,0:T(8,128)S(1)} %copy-done.4), kind=kOutput, calls=%fused_computation.29 | convolution fusion | flops 253837312 | bytes 8654848 | tf_op jit(solution)/shard_map/dot_general | solution.py:88
  137.3 22.5 %reduce.8 = bf16[4096,10]{1,0:T(8,128)(2,1)S(1)} reduce(bf16[4096,1,10]{2,1,0:T(2,128)(2,1)S(1)} %bitcast.171, bf16[]{:T(256)} %broadcast.396), dimensions={1}, to_apply=%bitcast.152.reduce_sub_computation | reduce | bytes 163842
  162.2 7.7 %all-to-all-start.1 = ((bf16[32,2,640]{2,1,0:T(2,128)(2,1)}), bf16[32,2,640]{2,1,0:T(2,128)(2,1)S(1)}, u32[]{:S(2)}, u32[]{:S(2)}) async-start(bf16[32,2,640]{2,1,0:T(2,128)(2,1)} %reshape.241), calls=%async_computation.1 | async-start | bytes 163840 | tf_op jit(solution)/shard_map/all_to_all | solution.py:175
  170.0 7.9 %all-to-all-done.1 = bf16[32,2,640]{2,1,0:T(2,128)(2,1)S(1)} async-done(((bf16[32,2,640]{2,1,0:T(2,128)(2,1)}), bf16[32,2,640]{2,1,0:T(2,128)(2,1)S(1)}, u32[]{:S(2)}, u32[]{:S(2)}) %all-to-all-start.1) | async-done | bytes 81952 | tf_op jit(solution)/shard_map/all_to_all | solution.py:175
  183.0 8.1 %all-to-all-start.2 = ((f32[8,3,4,128]{3,2,1,0:T(4,128)}), f32[8,3,4,128]{3,2,1,0:T(4,128)S(1)}, u32[]{:S(2)}, u32[]{:S(2)}) async-start(f32[8,3,4,128]{3,2,1,0:T(4,128)} %copy.29), calls=%async_computation.2 | async-start | bytes 98304 | tf_op jit(solution)/shard_map/all_to_all | solution.py:36
  191.2 9.1 %all-to-all-done.2 = f32[8,3,4,128]{3,2,1,0:T(4,128)S(1)} async-done(((f32[8,3,4,128]{3,2,1,0:T(4,128)}), f32[8,3,4,128]{3,2,1,0:T(4,128)S(1)}, u32[]{:S(2)}, u32[]{:S(2)}) %all-to-all-start.2) | async-done | bytes 49184 | tf_op jit(solution)/shard_map/all_to_all | solution.py:36
  200.6 7.2 %collective-permute-start.1 = (f32[3,4,128]{2,1,0:T(4,128)S(1)}, f32[3,4,128]{2,1,0:T(4,128)S(1)}, u32[]{:S(2)}, u32[]{:S(2)}) collective-permute-start(f32[3,4,128]{2,1,0:T(4,128)S(1)} %multiply_add_fusion.1), channel_id=1, source_target_pairs={{32,0},{64,32},{96,64},{128,96},{160,128},{192,160},{224,192},{0,2... | collective-permute-start | bytes 18440 | tf_op jit(solution)/shard_map/ppermute | solution.py:23
  212.3 6.9 %gather_fusion.2 = f32[1024]{0:T(1024)S(1)} fusion(f32[512]{0:T(512)S(1)} %slice_bitcast_fusion.36, s32[1024]{0:T(1024)S(1)} %get-tuple-element.30), kind=kCustom, calls=%fused_computation.2 | custom fusion | bytes 12288 | tf_op jit(solution)/shard_map/gather | solution.py:191
  220.0 6.9 %gather_fusion = f32[1024]{0:T(1024)S(1)} fusion(f32[512]{0:T(512)S(1)} %fusion.100, s32[1024]{0:T(1024)S(1)} %get-tuple-element.30), kind=kCustom, calls=%fused_computation | custom fusion | bytes 12288 | tf_op jit(solution)/shard_map/gather | solution.py:191
  226.9 6.9 %gather_fusion.1 = f32[1024]{0:T(1024)S(1)} fusion(f32[512]{0:T(512)S(1)} %slice_bitcast_fusion.37, s32[1024]{0:T(1024)S(1)} %get-tuple-element.30), kind=kCustom, calls=%fused_computation.1 | custom fusion | bytes 12288 | tf_op jit(solution)/shard_map/gather | solution.py:191
  233.8 7.6 %scatter_custom_fusion = f32[512]{0:T(512)S(1)} fusion(s32[1024]{0:T(1024)S(1)} %get-tuple-element.31, f32[1024]{0:T(1024)S(1)} %get-tuple-element.86, f32[]{:T(128)} %constant.182.clone.1), kind=kCustom, calls=%fused_computation.245 | custom fusion | flops 1024 | bytes 2052 | tf_op jit(solution)/shard_map/scatter-add | solution.py:198
  241.4 7.6 %scatter_custom_fusion.1 = f32[512]{0:T(512)S(1)} fusion(s32[1024]{0:T(1024)S(1)} %get-tuple-element.31, f32[1024]{0:T(1024)S(1)} %get-tuple-element.87, f32[]{:T(128)} %constant.182.clone.1), kind=kCustom, calls=%fused_computation.243 | custom fusion | flops 1024 | bytes 2052 | tf_op jit(solution)/shard_map/scatter-add | solution.py:198
  249.2 7.8 %collective-permute-start.5 = (f32[4,4,128]{2,1,0:T(4,128)S(1)}, f32[4,4,128]{2,1,0:T(4,128)S(1)}, u32[]{:S(2)}, u32[]{:S(2)}) collective-permute-start(f32[4,4,128]{2,1,0:T(4,128)S(1)} %pad_maximum_fusion.38), channel_id=1, source_target_pairs={{32,0},{64,32},{96,64},{128,96},{160,128},{192,160},{224,192},{0,2... | collective-permute-start | bytes 24584 | tf_op jit(solution)/shard_map/ppermute | solution.py:23
  264.5 7.6 %scatter_custom_fusion.2 = f32[512]{0:T(512)S(1)} fusion(s32[1024]{0:T(1024)S(1)} %get-tuple-element.31, f32[1024]{0:T(1024)S(1)} %get-tuple-element.26, f32[]{:T(128)} %constant.182.clone.1), kind=kCustom, calls=%fused_computation.241 | custom fusion | flops 1024 | bytes 2052 | tf_op jit(solution)/shard_map/scatter-add | solution.py:198
  273.6 17.9 %all_to_all.50 = bf16[8,3,4,128]{3,2,1,0:T(4,128)(2,1)S(1)} all-to-all(bf16[8,3,4,128]{3,2,1,0:T(4,128)(2,1)S(1)} %broadcast_in_dim.5), channel_id=1, replica_groups=mesh['grp'=8,'sp_0'=4,'sp_1'=4,'sp_2'=2] {'grp'}, dimensions={0} | all-to-all | bytes 49152 | tf_op jit(solution)/shard_map/all_to_all | solution.py:48
  291.8 20.8 %all_to_all.51 = f32[10,32,128]{2,0,1:T(8,128)S(1)} all-to-all(f32[10,32,128]{2,0,1:T(8,128)S(1)} %bitcast.180), channel_id=1, replica_groups=mesh['grp'=8,'sp_0'=4,'sp_1'=4,'sp_2'=2] {'sp_0','sp_1','sp_2'}, dimensions={1} | all-to-all | bytes 327680 | tf_op jit(solution)/shard_map/all_to_all | solution.py:173
  312.9 6.8 %fusion.51 = f32[10,512]{1,0:T(8,128)S(1)} fusion(f32[10,4096]{1,0:T(8,128)S(1)} %bitcast.173, f32[4096,256]{1,0:T(8,128)} %get-tuple-element.93, f32[4096,256]{1,0:T(8,128)} %get-tuple-element.92, f32[512]{0:T(512)S(1)} %get-tuple-element.101), kind=kOutput, calls=%fused_computation.79 | convolution fusion | flops 253760512 | bytes 8574976 | tf_op jit(solution)/shard_map/dot_general | solution.py:82
  327.9 4.5 %fusion.45 = f32[10,512]{1,0:T(8,128)S(1)} fusion(f32[10,4096]{1,0:T(8,128)S(1)} %bitcast.176, f32[4096,256]{1,0:T(8,128)S(1)} %copy-done.1, f32[4096,256]{1,0:T(8,128)S(1)} %copy-done.3, f32[512]{0:T(512)S(1)} %get-tuple-element.98), kind=kOutput, calls=%fused_computation.73 | convolution fusion | flops 253760512 | bytes 8574976 | tf_op jit(solution)/shard_map/dot_general | solution.py:82
  332.5 7.0 %fusion.32 = f32[10,4096]{1,0:T(8,128)S(1)} fusion(f32[10,512]{1,0:T(8,128)S(1)} %fusion.45, f32[4096,256]{1,0:T(8,128)S(1)} %copy-done.1, f32[4096,256]{1,0:T(8,128)S(1)} %copy-done.3), kind=kOutput, calls=%fused_computation.60 | convolution fusion | flops 253755392 | bytes 8572928 | tf_op jit(solution)/shard_map/dot_general | solution.py:88
  339.5 7.2 %convolution_add_fusion.2 = f32[10,4096]{1,0:T(8,128)S(1)} fusion(f32[10,4096]{1,0:T(8,128)S(1)} %fusion.32, f32[10,512]{1,0:T(8,128)S(1)} %fusion.47, f32[4096,256]{1,0:T(8,128)S(1)} %copy-done.15, f32[4096,256]{1,0:T(8,128)S(1)} %copy-done.13), kind=kOutput, calls=%fused_computation.24 | convolution fusion | flops 253796352 | bytes 8736768 | tf_op jit(solution)/shard_map/dot_general | solution.py:88
  346.7 7.0 %convolution_add_fusion.1 = f32[10,4096]{1,0:T(8,128)S(1)} fusion(f32[10,4096]{1,0:T(8,128)S(1)} %convolution_add_fusion.2, f32[10,512]{1,0:T(8,128)S(1)} %fusion.49, f32[4096,256]{1,0:T(8,128)S(1)} %copy-done.11, f32[4096,256]{1,0:T(8,128)S(1)} %copy-done.9), kind=kOutput, calls=%fused_computation.23 | convolution fusion | flops 253796352 | bytes 8736768 | tf_op jit(solution)/shard_map/dot_general | solution.py:88
  353.7 7.0 %convolution_add_fusion = f32[10,4096]{1,0:T(8,128)S(1)} fusion(f32[10,4096]{1,0:T(8,128)S(1)} %convolution_add_fusion.1, f32[10,512]{1,0:T(8,128)S(1)} %fusion.51, f32[4096,256]{1,0:T(8,128)S(1)} %copy-done.7, f32[4096,256]{1,0:T(8,128)S(1)} %copy-done.5), kind=kOutput, calls=%fused_computation.22 | convolution fusion | flops 253796352 | bytes 8736768 | tf_op jit(solution)/shard_map/dot_general | solution.py:88
  364.7 11.2 %all_to_all.53 = f32[16,2,10,1,128]{4,1,2,3,0:T(2,128)S(1)} all-to-all(f32[16,2,10,1,128]{4,1,2,3,0:T(2,128)S(1)} %copy.33), channel_id=1, replica_groups=mesh['grp'=8,'sp_0'=4,'sp_1'=4,'sp_2'=2] {'sp_0','sp_1'}, dimensions={0} | all-to-all | bytes 327680 | tf_op jit(solution)/shard_map/all_to_all | solution.py:59
  (153 shorter events, 54.6 us)
Async XLA Ops:
  2.4 81.4 %all-to-all-start = ((f32[10,32,128]{2,0,1:T(8,128)}), f32[10,32,128]{2,0,1:T(8,128)S(1)}, u32[]{:S(2)}, u32[]{:S(2)}) async-start(f32[10,32,128]{2,0,1:T(8,128)} %copy.25), calls=%async_computation | async-start | bytes 524288 | tf_op jit(solution)/shard_map/all_to_all | solution.py:173
  12.4 17.7 %copy-start.23 = (f32[1024]{0:T(1024)S(1)}, f32[1024]{0:T(1024)}, u32[]{:S(2)}) copy-start(f32[1024]{0:T(1024)} %param.17) | copy-start | bytes 12292
  65.8 17.9 %copy-start.24 = (s32[1024]{0:T(1024)S(1)}, s32[1024]{0:T(1024)}, u32[]{:S(2)}) copy-start(s32[1024]{0:T(1024)} %param.18) | copy-start | bytes 12292
  84.1 7.5 %copy-start = (f32[4096,256]{1,0:T(8,128)S(1)}, f32[4096,256]{1,0:T(8,128)}, u32[]{:S(2)}) copy-start(f32[4096,256]{1,0:T(8,128)} %get-tuple-element.102) | copy-start | bytes 12582916
  84.1 7.5 %copy-start.2 = (f32[4096,256]{1,0:T(8,128)S(1)}, f32[4096,256]{1,0:T(8,128)}, u32[]{:S(2)}) copy-start(f32[4096,256]{1,0:T(8,128)} %get-tuple-element.103) | copy-start | bytes 12582916
  91.6 7.0 %copy-start.12 = (f32[4096,256]{1,0:T(8,128)S(1)}, f32[4096,256]{1,0:T(8,128)}, u32[]{:S(2)}) copy-start(f32[4096,256]{1,0:T(8,128)} %get-tuple-element.96) | copy-start | bytes 12582916
  91.6 7.0 %copy-start.14 = (f32[4096,256]{1,0:T(8,128)S(1)}, f32[4096,256]{1,0:T(8,128)}, u32[]{:S(2)}) copy-start(f32[4096,256]{1,0:T(8,128)} %get-tuple-element.97) | copy-start | bytes 12582916
  103.1 7.2 %copy-start.8 = (f32[4096,256]{1,0:T(8,128)S(1)}, f32[4096,256]{1,0:T(8,128)}, u32[]{:S(2)}) copy-start(f32[4096,256]{1,0:T(8,128)} %get-tuple-element.94) | copy-start | bytes 12582916
  103.1 7.2 %copy-start.10 = (f32[4096,256]{1,0:T(8,128)S(1)}, f32[4096,256]{1,0:T(8,128)}, u32[]{:S(2)}) copy-start(f32[4096,256]{1,0:T(8,128)} %get-tuple-element.95) | copy-start | bytes 12582916
  114.8 7.2 %copy-start.4 = (f32[4096,256]{1,0:T(8,128)S(1)}, f32[4096,256]{1,0:T(8,128)}, u32[]{:S(2)}) copy-start(f32[4096,256]{1,0:T(8,128)} %get-tuple-element.92) | copy-start | bytes 12582916
  114.8 7.2 %copy-start.6 = (f32[4096,256]{1,0:T(8,128)S(1)}, f32[4096,256]{1,0:T(8,128)}, u32[]{:S(2)}) copy-start(f32[4096,256]{1,0:T(8,128)} %get-tuple-element.93) | copy-start | bytes 12582916
  137.3 45.0 %copy-start.16 = (bf16[10,3,32,128]{3,2,1,0:T(8,128)(2,1)S(1)}, bf16[10,3,32,128]{3,2,1,0:T(8,128)(2,1)}, u32[]{:S(2)}) copy-start(bf16[10,3,32,128]{3,2,1,0:T(8,128)(2,1)} %param.14) | copy-start | bytes 737284
  159.8 40.5 %copy-start.18 = (f32[3,4,128]{2,1,0:T(4,128)S(1)}, f32[3,4,128]{2,1,0:T(4,128)}, u32[]{:S(2)}) copy-start(f32[3,4,128]{2,1,0:T(4,128)} %param.16) | copy-start | bytes 18436
  159.8 40.5 %copy-start.19 = (f32[3,4,128]{2,1,0:T(4,128)S(1)}, f32[3,4,128]{2,1,0:T(4,128)}, u32[]{:S(2)}) copy-start(f32[3,4,128]{2,1,0:T(4,128)} %param.15) | copy-start | bytes 18436
  162.2 15.6 %all-to-all-start.1 = ((bf16[32,2,640]{2,1,0:T(2,128)(2,1)}), bf16[32,2,640]{2,1,0:T(2,128)(2,1)S(1)}, u32[]{:S(2)}, u32[]{:S(2)}) async-start(bf16[32,2,640]{2,1,0:T(2,128)(2,1)} %reshape.241), calls=%async_computation.1 | async-start | bytes 163840 | tf_op jit(solution)/shard_map/all_to_all | solution.py:175
  183.0 17.2 %all-to-all-start.2 = ((f32[8,3,4,128]{3,2,1,0:T(4,128)}), f32[8,3,4,128]{3,2,1,0:T(4,128)S(1)}, u32[]{:S(2)}, u32[]{:S(2)}) async-start(f32[8,3,4,128]{3,2,1,0:T(4,128)} %copy.29), calls=%async_computation.2 | async-start | bytes 98304 | tf_op jit(solution)/shard_map/all_to_all | solution.py:36
  200.3 8.6 %collective-permute-start = (f32[3,4,128]{2,1,0:T(4,128)S(1)}, f32[3,4,128]{2,1,0:T(4,128)S(1)}, u32[]{:S(2)}, u32[]{:S(2)}) collective-permute-start(f32[3,4,128]{2,1,0:T(4,128)S(1)} %multiply_add_fusion.1), channel_id=1, source_target_pairs={{0,32},{32,64},{64,96},{96,128},{128,160},{160,192},{192,224},{224... | collective-permute-start | bytes 18440 | tf_op jit(solution)/shard_map/ppermute | solution.py:20
  200.6 8.2 %collective-permute-start.1 = (f32[3,4,128]{2,1,0:T(4,128)S(1)}, f32[3,4,128]{2,1,0:T(4,128)S(1)}, u32[]{:S(2)}, u32[]{:S(2)}) collective-permute-start(f32[3,4,128]{2,1,0:T(4,128)S(1)} %multiply_add_fusion.1), channel_id=1, source_target_pairs={{32,0},{64,32},{96,64},{128,96},{160,128},{192,160},{224,192},{0,2... | collective-permute-start | bytes 18440 | tf_op jit(solution)/shard_map/ppermute | solution.py:23
  208.9 10.2 %collective-permute-start.2 = (f32[3,12,4]{2,1,0:T(8,128)S(1)}, f32[3,12,4]{2,1,0:T(8,128)S(1)}, u32[]{:S(2)}, u32[]{:S(2)}) collective-permute-start(f32[3,12,4]{2,1,0:T(8,128)S(1)} %get-tuple-element.66), channel_id=1, source_target_pairs={{0,1},{1,2},{2,3},{3,4},{4,5},{5,6},{6,7},{7,8},{8,9},{9,10},{10,1... | collective-permute-start | bytes 1736 | tf_op jit(solution)/shard_map/ppermute | solution.py:20
  212.1 7.1 %collective-permute-start.3 = (f32[3,12,4]{2,1,0:T(8,128)S(1)}, f32[3,12,4]{2,1,0:T(8,128)S(1)}, u32[]{:S(2)}, u32[]{:S(2)}) collective-permute-start(f32[3,12,4]{2,1,0:T(8,128)S(1)} %get-tuple-element.67), channel_id=1, source_target_pairs={{1,0},{2,1},{3,2},{4,3},{5,4},{6,5},{7,6},{8,7},{9,8},{10,9},{11,1... | collective-permute-start | bytes 1736 | tf_op jit(solution)/shard_map/ppermute | solution.py:23
  220.0 13.8 %copy-start.20 = (f32[1024]{0:T(1024)S(1)}, f32[1024]{0:T(1024)}, u32[]{:S(2)}) copy-start(f32[1024]{0:T(1024)} %param.21) | copy-start | bytes 12292
  220.0 13.8 %copy-start.21 = (f32[1024]{0:T(1024)S(1)}, f32[1024]{0:T(1024)}, u32[]{:S(2)}) copy-start(f32[1024]{0:T(1024)} %param.20) | copy-start | bytes 12292
  220.0 13.8 %copy-start.22 = (s32[1024]{0:T(1024)S(1)}, s32[1024]{0:T(1024)}, u32[]{:S(2)}) copy-start(s32[1024]{0:T(1024)} %param.19) | copy-start | bytes 12292
  249.1 8.9 %collective-permute-start.4 = (f32[4,4,128]{2,1,0:T(4,128)S(1)}, f32[4,4,128]{2,1,0:T(4,128)S(1)}, u32[]{:S(2)}, u32[]{:S(2)}) collective-permute-start(f32[4,4,128]{2,1,0:T(4,128)S(1)} %pad_maximum_fusion.38), channel_id=1, source_target_pairs={{0,32},{32,64},{64,96},{96,128},{128,160},{160,192},{192,224},{224... | collective-permute-start | bytes 24584 | tf_op jit(solution)/shard_map/ppermute | solution.py:20
  249.2 8.8 %collective-permute-start.5 = (f32[4,4,128]{2,1,0:T(4,128)S(1)}, f32[4,4,128]{2,1,0:T(4,128)S(1)}, u32[]{:S(2)}, u32[]{:S(2)}) collective-permute-start(f32[4,4,128]{2,1,0:T(4,128)S(1)} %pad_maximum_fusion.38), channel_id=1, source_target_pairs={{32,0},{64,32},{96,64},{128,96},{160,128},{192,160},{224,192},{0,2... | collective-permute-start | bytes 24584 | tf_op jit(solution)/shard_map/ppermute | solution.py:23
  258.1 14.1 %collective-permute-start.6 = (f32[4,12,4]{2,1,0:T(8,128)S(1)}, f32[4,12,4]{2,1,0:T(8,128)S(1)}, u32[]{:S(2)}, u32[]{:S(2)}) collective-permute-start(f32[4,12,4]{2,1,0:T(8,128)S(1)} %get-tuple-element.48), channel_id=1, source_target_pairs={{0,1},{1,2},{2,3},{3,4},{4,5},{5,6},{6,7},{7,8},{8,9},{9,10},{10,1... | collective-permute-start | bytes 2312 | tf_op jit(solution)/shard_map/ppermute | solution.py:20
  260.7 11.5 %collective-permute-start.7 = (f32[4,12,4]{2,1,0:T(8,128)S(1)}, f32[4,12,4]{2,1,0:T(8,128)S(1)}, u32[]{:S(2)}, u32[]{:S(2)}) collective-permute-start(f32[4,12,4]{2,1,0:T(8,128)S(1)} %get-tuple-element.49), channel_id=1, source_target_pairs={{1,0},{2,1},{3,2},{4,3},{5,4},{6,5},{7,6},{8,7},{9,8},{10,9},{11,1... | collective-permute-start | bytes 2312 | tf_op jit(solution)/shard_map/ppermute | solution.py:23
  312.8 6.9 %copy-start.9 = (f32[4096,256]{1,0:T(8,128)S(1)}, f32[4096,256]{1,0:T(8,128)}, u32[]{:S(2)}) copy-start(f32[4096,256]{1,0:T(8,128)} %get-tuple-element.94) | copy-start | bytes 12582916
  312.9 6.9 %copy-start.11 = (f32[4096,256]{1,0:T(8,128)S(1)}, f32[4096,256]{1,0:T(8,128)}, u32[]{:S(2)}) copy-start(f32[4096,256]{1,0:T(8,128)} %get-tuple-element.95) | copy-start | bytes 12582916
  346.6 7.0 %copy-start.5 = (f32[4096,256]{1,0:T(8,128)S(1)}, f32[4096,256]{1,0:T(8,128)}, u32[]{:S(2)}) copy-start(f32[4096,256]{1,0:T(8,128)} %get-tuple-element.92) | copy-start | bytes 12582916
  346.7 7.0 %copy-start.7 = (f32[4096,256]{1,0:T(8,128)S(1)}, f32[4096,256]{1,0:T(8,128)}, u32[]{:S(2)}) copy-start(f32[4096,256]{1,0:T(8,128)} %get-tuple-element.93) | copy-start | bytes 12582916
  353.7 22.4 %copy-start.17 = (f32[10,32,128]{2,1,0:T(8,128)S(1)}, f32[10,32,128]{2,1,0:T(8,128)}, u32[]{:S(2)}) copy-start(f32[10,32,128]{2,1,0:T(8,128)} %param.13) | copy-start | bytes 491524
  (4 other events, 16.4 us)
where the time goes:
time: 383 us; the launch traced here: 377 us
  other arithmetic  120 us (31%)
  matrix products  97.4 us (25%)
  blocking collectives  53.7 us (14%)
  starting transfers between devices  51.1 us (13%)
  local copies, waits for them, and re-layouts  34.5 us (9%)
  waiting for transfers between devices  18.9 us (5%)
    dot_general x8, matrix products, spectral_filter(): jnp.dot(coeffs * weights[None, :], fourier_basis.T, precision=lax.Precisi...  56.9 us
    cos x3, other arithmetic, spectral_filter(): jnp.cos(radians)  53.6 us
    dot_general x8, matrix products, spectral_filter(): jnp.dot(rows_data, fourier_basis, precision=lax.Precision.HIGHEST, prefer...  40.5 us
    scatter-add x3, other arithmetic, per_device(): jnp.zeros((tile_rows * tile_cols,), jnp.float32).at[local_index]  22.8 us
    unnamed x4, other arithmetic  22.5 us
    all_to_all x1, blocking collectives, to_rows(): lax.all_to_all(columns, SP, split_axis=1, concat_axis=2, tiled=True)  20.8 us
    gather x3, local copies, waits for them, and re-layouts, per_device(): values = states[moment][0].reshape(-1)[local_index]  20.6 us
    ppermute x4, starting transfers between devices, extended(): lax.ppermute(lax.slice_in_dim(block, 0, width, axis=dim), axis, backward)  19 us
  transfers between devices with their start and end apart: 11, of which 4 were waited for; matrix products, arithmetic and copies ran while one was open for 23% of the time, Pallas kernels for 0%

commit v1 on v0

--- a/solution.py
+++ b/solution.py
@@ -172,8 +172,14 @@
     def to_rows(columns):
         return localize_items(lax.all_to_all(columns, SP, split_axis=1, concat_axis=2, tiled=True))
 
-    localized = lax.all_to_all(
-        to_rows(alpha).astype(jnp.bfloat16), SP, split_axis=2, concat_axis=1, tiled=True
+    localized = jnp.concatenate(
+        lax.all_to_all(
+            jnp.stack(jnp.split(to_rows(alpha).astype(jnp.bfloat16), lax.axis_size(SP), axis=2)),
+            SP,
+            0,
+            0,
+        ),
+        axis=1,
     )
     partial_value = jnp.einsum(
         "mvyx,myx->vyx", ensemble, localized, preferred_element_type=jnp.float32

time: 383 us -> 369 us (0.963)
  other arithmetic: 120 us -> 97.2 us
  waiting for transfers between devices: 18.9 us -> 33.1 us
  starting transfers between devices: 51.1 us -> 38.8 us
  local copies, waits for them, and re-layouts: 34.5 us -> 43.4 us
    unnamed x4 -> x3, other arithmetic: 22.5 us -> 0.08 us
    ppermute x4, starting transfers between devices: 19 us -> 5.29 us  [extended(): lax.ppermute(lax.slice_in_dim(block, 0, width, axis=dim), axis, backward)]
    unnamed x60 -> x88, local copies, waits for them, and re-layouts: 7.55 us -> 20.8 us
    ppermute x4, waiting for transfers between devices: 1.96 us -> 13.4 us  [extended(): lax.ppermute(lax.slice_in_dim(block, block.shape[dim] - width, None, axis...]
  transfers between devices with their start and end apart: 11 -> 11, of which waited for: 4 -> 6; matrix products, arithmetic and copies ran while one was open for 23% -> 24% of each run, Pallas kernels for 0% -> 0%
where the time goes in v1:
time: 369 us; the launch traced here: 362 us
  matrix products  97.3 us (26%)
  other arithmetic  97.2 us (26%)
  blocking collectives  50.8 us (14%)
  local copies, waits for them, and re-layouts  43.4 us (12%)
  starting transfers between devices  38.8 us (11%)
  waiting for transfers between devices  33.1 us (9%)
    dot_general x8, matrix products, spectral_filter(): jnp.dot(coeffs * weights[None, :], fourier_basis.T, precision=lax.Precisi...  56.9 us
    cos x3, other arithmetic, spectral_filter(): jnp.cos(radians)  53.6 us
    dot_general x8, matrix products, spectral_filter(): jnp.dot(rows_data, fourier_basis, precision=lax.Precision.HIGHEST, prefer...  40.4 us
    scatter-add x3, other arithmetic, per_device(): jnp.zeros((tile_rows * tile_cols,), jnp.float32).at[local_index]  22.8 us
    all_to_all x1, blocking collectives, to_rows(): lax.all_to_all(columns, SP, split_axis=1, concat_axis=2, tiled=True)  20.8 us
    unnamed x88, local copies, waits for them, and re-layouts  20.8 us
    gather x3, local copies, waits for them, and re-layouts, per_device(): values = states[moment][0].reshape(-1)[local_index]  20.6 us
    sin x1, other arithmetic, spectral_filter(): jnp.sin(radians)  17.6 us
  transfers between devices with their start and end apart: 11, of which 6 were waited for; matrix products, arithmetic and copies ran while one was open for 24% of the time, Pallas kernels for 0%

profile of v1, /device:TPU:1, one launch (start us, length us, event | category | flops | bytes accessed | tf_op | source)
XLA Modules:
  0.0 362.3 jit_solution(2236273542922296528)
XLA Ops:
  2.4 10.0 %all-to-all-start = ((f32[10,32,128]{2,0,1:T(8,128)}), f32[10,32,128]{2,0,1:T(8,128)S(1)}, u32[]{:S(2)}, u32[]{:S(2)}) async-start(f32[10,32,128]{2,0,1:T(8,128)} %copy.22), calls=%async_computation | async-start | bytes 524288 | tf_op jit(solution)/shard_map/all_to_all | solution.py:173
  12.5 17.6 %fusion.36 = (f32[4096,256]{1,0:T(8,128)}, f32[4096,256]{1,0:T(8,128)}) fusion(), kind=kLoop, calls=%fused_computation.64 | loop fusion | flops 14680064 | bytes 8388608 | tf_op jit(solution)/shard_map/sin | solution.py:79
  30.1 17.9 %fusion.39 = (f32[4096,256]{1,0:T(8,128)}, f32[4096,256]{1,0:T(8,128)}) fusion(s32[256]{0:T(256)S(1)} %iota_add_fusion), kind=kLoop, calls=%fused_computation.67 | loop fusion | flops 14680064 | bytes 8389632 | tf_op jit(solution)/shard_map/cos | solution.py:79
  47.9 17.9 %fusion.41 = (f32[4096,256]{1,0:T(8,128)}, f32[4096,256]{1,0:T(8,128)}) fusion(s32[256]{0:T(256)S(1)} %iota_add_fusion.1), kind=kLoop, calls=%fused_computation.69 | loop fusion | flops 14680064 | bytes 8389632 | tf_op jit(solution)/shard_map/cos | solution.py:79
  65.8 17.9 %fusion.43 = (f32[4096,256]{1,0:T(8,128)}, f32[4096,256]{1,0:T(8,128)}) fusion(s32[256]{0:T(256)S(1)} %iota_add_fusion.2), kind=kLoop, calls=%fused_computation.71 | loop fusion | flops 14680064 | bytes 8389632 | tf_op jit(solution)/shard_map/cos | solution.py:79
  84.1 7.5 %fusion.44 = f32[512,10]{0,1:T(8,128)S(1)} fusion(f32[10,4096]{1,0:T(8,128)S(1)} %bitcast.305, f32[4096,256]{1,0:T(8,128)} %get-tuple-element.102, f32[4096,256]{1,0:T(8,128)} %get-tuple-element.103, f32[512]{0:T(512)S(1)} %get-tuple-element.98), kind=kOutput, calls=%fused_computation.72 | convolution fusion | flops 253760512 | bytes 8574976 | tf_op jit(solution)/shard_map/dot_general | solution.py:82
  91.6 7.0 %fusion.34 = f32[10,4096]{1,0:T(8,128)S(1)} fusion(f32[512,10]{0,1:T(8,128)S(1)} %fusion.44, f32[4096,256]{1,0:T(8,128)S(1)} %copy-done, f32[4096,256]{1,0:T(8,128)S(1)} %copy-done.2), kind=kOutput, calls=%fused_computation.62 | convolution fusion | flops 253755392 | bytes 8572928 | tf_op jit(solution)/shard_map/dot_general | solution.py:88
  98.6 4.5 %fusion.46 = f32[512,10]{0,1:T(8,128)S(1)} fusion(f32[10,4096]{1,0:T(8,128)S(1)} %bitcast.306, f32[4096,256]{1,0:T(8,128)S(1)} %copy-done.14, f32[4096,256]{1,0:T(8,128)S(1)} %copy-done.12, f32[512]{0:T(512)S(1)} %get-tuple-element.99), kind=kOutput, calls=%fused_computation.74 | convolution fusion | flops 253760512 | bytes 8574976 | tf_op jit(solution)/shard_map/dot_general | solution.py:82
  103.1 7.2 %convolution_add_fusion.5 = f32[10,4096]{1,0:T(8,128)S(1)} fusion(f32[10,4096]{1,0:T(8,128)S(1)} %fusion.34, f32[512,10]{0,1:T(8,128)S(1)} %fusion.46, f32[4096,256]{1,0:T(8,128)S(1)} %copy-done.14, f32[4096,256]{1,0:T(8,128)S(1)} %copy-done.12), kind=kOutput, calls=%fused_computation.27 | convolution fusion | flops 253796352 | bytes 8736768 | tf_op jit(solution)/shard_map/dot_general | solution.py:88
  110.3 4.5 %fusion.48 = f32[512,10]{0,1:T(8,128)S(1)} fusion(f32[10,4096]{1,0:T(8,128)S(1)} %bitcast.307, f32[4096,256]{1,0:T(8,128)S(1)} %copy-done.10, f32[4096,256]{1,0:T(8,128)S(1)} %copy-done.8, f32[512]{0:T(512)S(1)} %get-tuple-element.100), kind=kOutput, calls=%fused_computation.76 | convolution fusion | flops 253760512 | bytes 8574976 | tf_op jit(solution)/shard_map/dot_general | solution.py:82
  114.8 7.4 %convolution_add_fusion.4 = f32[10,4096]{1,0:T(8,128)S(1)} fusion(f32[10,4096]{1,0:T(8,128)S(1)} %convolution_add_fusion.5, f32[512,10]{0,1:T(8,128)S(1)} %fusion.48, f32[4096,256]{1,0:T(8,128)S(1)} %copy-done.10, f32[4096,256]{1,0:T(8,128)S(1)} %copy-done.8), kind=kOutput, calls=%fused_computation.26 | convolution fusion | flops 253796352 | bytes 8736768 | tf_op jit(solution)/shard_map/dot_general | solution.py:88
  126.8 7.2 %fusion.1 = bf16[10,1,4096]{2,0,1:T(8,128)(2,1)S(1)} fusion(f32[10,4096]{1,0:T(8,128)S(1)} %convolution_add_fusion.4, f32[512,10]{0,1:T(8,128)S(1)} %fusion.50, f32[4096,256]{1,0:T(8,128)S(1)} %copy-done.6, f32[4096,256]{1,0:T(8,128)S(1)} %copy-done.4), kind=kOutput, calls=%fused_computation.29 | convolution fusion | flops 253837312 | bytes 8654848 | tf_op jit(solution)/shard_map/dot_general | solution.py:88
  153.0 7.7 %all-to-all-start.1 = ((bf16[32,10,1,128]{3,1,2,0:T(8,128)(2,1)}), bf16[32,10,1,128]{3,1,2,0:T(8,128)(2,1)S(1)}, u32[]{:S(2)}, u32[]{:S(2)}) async-start(bf16[32,10,1,128]{3,1,2,0:T(8,128)(2,1)} %constant_dynamic-update-slice_fusion), calls=%async_computation.1 | async-start | bytes 262144 | tf_op jit(solution)/shard_map/all_to_all | solution.py:176
  160.8 8.5 %all-to-all-done.1 = bf16[32,10,1,128]{3,1,2,0:T(8,128)(2,1)S(1)} async-done(((bf16[32,10,1,128]{3,1,2,0:T(8,128)(2,1)}), bf16[32,10,1,128]{3,1,2,0:T(8,128)(2,1)S(1)}, u32[]{:S(2)}, u32[]{:S(2)}) %all-to-all-start.1) | async-done | bytes 81952 | tf_op jit(solution)/shard_map/all_to_all | solution.py:176
  170.1 8.1 %all-to-all-start.2 = ((f32[8,3,4,128]{3,2,1,0:T(4,128)}), f32[8,3,4,128]{3,2,1,0:T(4,128)S(1)}, u32[]{:S(2)}, u32[]{:S(2)}) async-start(f32[8,3,4,128]{3,2,1,0:T(4,128)} %copy.24), calls=%async_computation.2 | async-start | bytes 98304 | tf_op jit(solution)/shard_map/all_to_all | solution.py:36
  178.2 9.1 %all-to-all-done.2 = f32[8,3,4,128]{3,2,1,0:T(4,128)S(1)} async-done(((f32[8,3,4,128]{3,2,1,0:T(4,128)}), f32[8,3,4,128]{3,2,1,0:T(4,128)S(1)}, u32[]{:S(2)}, u32[]{:S(2)}) %all-to-all-start.2) | async-done | bytes 49184 | tf_op jit(solution)/shard_map/all_to_all | solution.py:36
  189.9 7.3 %collective-permute-done = f32[3,4,128]{2,1,0:T(4,128)S(1)} collective-permute-done((f32[3,4,128]{2,1,0:T(4,128)S(1)}, f32[3,4,128]{2,1,0:T(4,128)S(1)}, u32[]{:S(2)}, u32[]{:S(2)}) %collective-permute-start) | collective-permute-done | bytes 6176 | tf_op jit(solution)/shard_map/ppermute | solution.py:20
  200.5 6.9 %gather_fusion.2 = f32[1024]{0:T(1024)S(1)} fusion(f32[512]{0:T(512)S(1)} %slice_bitcast_fusion.67, s32[1024]{0:T(1024)S(1)} %get-tuple-element.30), kind=kCustom, calls=%fused_computation.2 | custom fusion | bytes 12288 | tf_op jit(solution)/shard_map/gather | solution.py:197
  208.2 6.9 %gather_fusion = f32[1024]{0:T(1024)S(1)} fusion(f32[512]{0:T(512)S(1)} %fusion.99, s32[1024]{0:T(1024)S(1)} %get-tuple-element.30), kind=kCustom, calls=%fused_computation | custom fusion | bytes 12288 | tf_op jit(solution)/shard_map/gather | solution.py:197
  215.1 6.9 %gather_fusion.1 = f32[1024]{0:T(1024)S(1)} fusion(f32[512]{0:T(512)S(1)} %slice_bitcast_fusion.68, s32[1024]{0:T(1024)S(1)} %get-tuple-element.30), kind=kCustom, calls=%fused_computation.1 | custom fusion | bytes 12288 | tf_op jit(solution)/shard_map/gather | solution.py:197
  222.0 7.6 %scatter_custom_fusion = f32[512]{0:T(512)S(1)} fusion(s32[1024]{0:T(1024)S(1)} %get-tuple-element.31, f32[1024]{0:T(1024)S(1)} %get-tuple-element.86, f32[]{:T(128)} %constant.182.clone.1), kind=kCustom, calls=%fused_computation.308 | custom fusion | flops 1024 | bytes 2052 | tf_op jit(solution)/shard_map/scatter-add | solution.py:204
  229.6 7.6 %scatter_custom_fusion.1 = f32[512]{0:T(512)S(1)} fusion(s32[1024]{0:T(1024)S(1)} %get-tuple-element.31, f32[1024]{0:T(1024)S(1)} %get-tuple-element.87, f32[]{:T(128)} %constant.182.clone.1), kind=kCustom, calls=%fused_computation.306 | custom fusion | flops 1024 | bytes 2052 | tf_op jit(solution)/shard_map/scatter-add | solution.py:204
  239.9 6.1 %collective-permute-done.4 = f32[4,4,128]{2,1,0:T(4,128)S(1)} collective-permute-done((f32[4,4,128]{2,1,0:T(4,128)S(1)}, f32[4,4,128]{2,1,0:T(4,128)S(1)}, u32[]{:S(2)}, u32[]{:S(2)}) %collective-permute-start.4) | collective-permute-done | bytes 8224 | tf_op jit(solution)/shard_map/ppermute | solution.py:20
  252.8 7.6 %scatter_custom_fusion.2 = f32[512]{0:T(512)S(1)} fusion(s32[1024]{0:T(1024)S(1)} %get-tuple-element.31, f32[1024]{0:T(1024)S(1)} %get-tuple-element.26, f32[]{:T(128)} %constant.182.clone.1), kind=kCustom, calls=%fused_computation.304 | custom fusion | flops 1024 | bytes 2052 | tf_op jit(solution)/shard_map/scatter-add | solution.py:204
  261.9 15.0 %all_to_all.43 = bf16[8,3,4,128]{3,2,1,0:T(4,128)(2,1)S(1)} all-to-all(bf16[8,3,4,128]{3,2,1,0:T(4,128)(2,1)S(1)} %broadcast_in_dim.5), channel_id=1, replica_groups=mesh['grp'=8,'sp_0'=4,'sp_1'=4,'sp_2'=2] {'grp'}, dimensions={0} | all-to-all | bytes 49152 | tf_op jit(solution)/shard_map/all_to_all | solution.py:48
  277.1 20.8 %all_to_all.44 = f32[10,32,128]{2,0,1:T(8,128)S(1)} all-to-all(f32[10,32,128]{2,0,1:T(8,128)S(1)} %bitcast.301), channel_id=1, replica_groups=mesh['grp'=8,'sp_0'=4,'sp_1'=4,'sp_2'=2] {'sp_0','sp_1','sp_2'}, dimensions={1} | all-to-all | bytes 327680 | tf_op jit(solution)/shard_map/all_to_all | solution.py:173
  298.3 7.0 %fusion.51 = f32[10,512]{1,0:T(8,128)S(1)} fusion(f32[10,4096]{1,0:T(8,128)S(1)} %bitcast.294, f32[4096,256]{1,0:T(8,128)} %get-tuple-element.93, f32[4096,256]{1,0:T(8,128)} %get-tuple-element.92, f32[512]{0:T(512)S(1)} %get-tuple-element.101), kind=kOutput, calls=%fused_computation.79 | convolution fusion | flops 253760512 | bytes 8574976 | tf_op jit(solution)/shard_map/dot_general | solution.py:82
  317.8 7.0 %fusion.32 = f32[10,4096]{1,0:T(8,128)S(1)} fusion(f32[10,512]{1,0:T(8,128)S(1)} %fusion.45, f32[4096,256]{1,0:T(8,128)S(1)} %copy-done.1, f32[4096,256]{1,0:T(8,128)S(1)} %copy-done.3), kind=kOutput, calls=%fused_computation.60 | convolution fusion | flops 253755392 | bytes 8572928 | tf_op jit(solution)/shard_map/dot_general | solution.py:88
  324.8 7.2 %convolution_add_fusion.2 = f32[10,4096]{1,0:T(8,128)S(1)} fusion(f32[10,4096]{1,0:T(8,128)S(1)} %fusion.32, f32[10,512]{1,0:T(8,128)S(1)} %fusion.47, f32[4096,256]{1,0:T(8,128)S(1)} %copy-done.15, f32[4096,256]{1,0:T(8,128)S(1)} %copy-done.13), kind=kOutput, calls=%fused_computation.24 | convolution fusion | flops 253796352 | bytes 8736768 | tf_op jit(solution)/shard_map/dot_general | solution.py:88
  332.0 7.0 %convolution_add_fusion.1 = f32[10,4096]{1,0:T(8,128)S(1)} fusion(f32[10,4096]{1,0:T(8,128)S(1)} %convolution_add_fusion.2, f32[10,512]{1,0:T(8,128)S(1)} %fusion.49, f32[4096,256]{1,0:T(8,128)S(1)} %copy-done.11, f32[4096,256]{1,0:T(8,128)S(1)} %copy-done.9), kind=kOutput, calls=%fused_computation.23 | convolution fusion | flops 253796352 | bytes 8736768 | tf_op jit(solution)/shard_map/dot_general | solution.py:88
  339.0 7.0 %convolution_add_fusion = f32[10,4096]{1,0:T(8,128)S(1)} fusion(f32[10,4096]{1,0:T(8,128)S(1)} %convolution_add_fusion.1, f32[10,512]{1,0:T(8,128)S(1)} %fusion.51, f32[4096,256]{1,0:T(8,128)S(1)} %copy-done.7, f32[4096,256]{1,0:T(8,128)S(1)} %copy-done.5), kind=kOutput, calls=%fused_computation.22 | convolution fusion | flops 253796352 | bytes 8736768 | tf_op jit(solution)/shard_map/dot_general | solution.py:88
  350.0 11.2 %all_to_all.46 = f32[16,2,10,1,128]{4,1,2,3,0:T(2,128)S(1)} all-to-all(f32[16,2,10,1,128]{4,1,2,3,0:T(2,128)S(1)} %copy.28), channel_id=1, replica_groups=mesh['grp'=8,'sp_0'=4,'sp_1'=4,'sp_2'=2] {'sp_0','sp_1'}, dimensions={0} | all-to-all | bytes 327680 | tf_op jit(solution)/shard_map/all_to_all | solution.py:59
  (179 shorter events, 61.7 us)
Async XLA Ops:
  2.4 81.4 %all-to-all-start = ((f32[10,32,128]{2,0,1:T(8,128)}), f32[10,32,128]{2,0,1:T(8,128)S(1)}, u32[]{:S(2)}, u32[]{:S(2)}) async-start(f32[10,32,128]{2,0,1:T(8,128)} %copy.22), calls=%async_computation | async-start | bytes 524288 | tf_op jit(solution)/shard_map/all_to_all | solution.py:173
  12.5 17.6 %copy-start.23 = (f32[1024]{0:T(1024)S(1)}, f32[1024]{0:T(1024)}, u32[]{:S(2)}) copy-start(f32[1024]{0:T(1024)} %param.17) | copy-start | bytes 12292
  65.8 17.9 %copy-start.24 = (s32[1024]{0:T(1024)S(1)}, s32[1024]{0:T(1024)}, u32[]{:S(2)}) copy-start(s32[1024]{0:T(1024)} %param.18) | copy-start | bytes 12292
  84.0 7.5 %copy-start = (f32[4096,256]{1,0:T(8,128)S(1)}, f32[4096,256]{1,0:T(8,128)}, u32[]{:S(2)}) copy-start(f32[4096,256]{1,0:T(8,128)} %get-tuple-element.102) | copy-start | bytes 12582916
  84.0 7.5 %copy-start.2 = (f32[4096,256]{1,0:T(8,128)S(1)}, f32[4096,256]{1,0:T(8,128)}, u32[]{:S(2)}) copy-start(f32[4096,256]{1,0:T(8,128)} %get-tuple-element.103) | copy-start | bytes 12582916
  91.6 7.0 %copy-start.12 = (f32[4096,256]{1,0:T(8,128)S(1)}, f32[4096,256]{1,0:T(8,128)}, u32[]{:S(2)}) copy-start(f32[4096,256]{1,0:T(8,128)} %get-tuple-element.96) | copy-start | bytes 12582916
  91.6 7.0 %copy-start.14 = (f32[4096,256]{1,0:T(8,128)S(1)}, f32[4096,256]{1,0:T(8,128)}, u32[]{:S(2)}) copy-start(f32[4096,256]{1,0:T(8,128)} %get-tuple-element.97) | copy-start | bytes 12582916
  103.1 7.2 %copy-start.8 = (f32[4096,256]{1,0:T(8,128)S(1)}, f32[4096,256]{1,0:T(8,128)}, u32[]{:S(2)}) copy-start(f32[4096,256]{1,0:T(8,128)} %get-tuple-element.94) | copy-start | bytes 12582916
  103.1 7.2 %copy-start.10 = (f32[4096,256]{1,0:T(8,128)S(1)}, f32[4096,256]{1,0:T(8,128)}, u32[]{:S(2)}) copy-start(f32[4096,256]{1,0:T(8,128)} %get-tuple-element.95) | copy-start | bytes 12582916
  114.8 7.4 %copy-start.4 = (f32[4096,256]{1,0:T(8,128)S(1)}, f32[4096,256]{1,0:T(8,128)}, u32[]{:S(2)}) copy-start(f32[4096,256]{1,0:T(8,128)} %get-tuple-element.92) | copy-start | bytes 12582916
  114.8 7.4 %copy-start.6 = (f32[4096,256]{1,0:T(8,128)S(1)}, f32[4096,256]{1,0:T(8,128)}, u32[]{:S(2)}) copy-start(f32[4096,256]{1,0:T(8,128)} %get-tuple-element.93) | copy-start | bytes 12582916
  126.7 42.6 %copy-start.16 = (bf16[10,3,32,128]{3,2,1,0:T(8,128)(2,1)S(1)}, bf16[10,3,32,128]{3,2,1,0:T(8,128)(2,1)}, u32[]{:S(2)}) copy-start(bf16[10,3,32,128]{3,2,1,0:T(8,128)(2,1)} %param.14) | copy-start | bytes 737284
  126.8 60.5 %copy-start.18 = (f32[3,4,128]{2,1,0:T(4,128)S(1)}, f32[3,4,128]{2,1,0:T(4,128)}, u32[]{:S(2)}) copy-start(f32[3,4,128]{2,1,0:T(4,128)} %param.16) | copy-start | bytes 18436
  126.8 60.5 %copy-start.19 = (f32[3,4,128]{2,1,0:T(4,128)S(1)}, f32[3,4,128]{2,1,0:T(4,128)}, u32[]{:S(2)}) copy-start(f32[3,4,128]{2,1,0:T(4,128)} %param.15) | copy-start | bytes 18436
  153.0 16.3 %all-to-all-start.1 = ((bf16[32,10,1,128]{3,1,2,0:T(8,128)(2,1)}), bf16[32,10,1,128]{3,1,2,0:T(8,128)(2,1)S(1)}, u32[]{:S(2)}, u32[]{:S(2)}) async-start(bf16[32,10,1,128]{3,1,2,0:T(8,128)(2,1)} %constant_dynamic-update-slice_fusion), calls=%async_computation.1 | async-start | bytes 262144 | tf_op jit(solution)/shard_map/all_to_all | solution.py:176
  170.1 17.2 %all-to-all-start.2 = ((f32[8,3,4,128]{3,2,1,0:T(4,128)}), f32[8,3,4,128]{3,2,1,0:T(4,128)S(1)}, u32[]{:S(2)}, u32[]{:S(2)}) async-start(f32[8,3,4,128]{3,2,1,0:T(4,128)} %copy.24), calls=%async_computation.2 | async-start | bytes 98304 | tf_op jit(solution)/shard_map/all_to_all | solution.py:36
  187.3 2.6 collective-permute-start.1
  188.7 8.5 %collective-permute-start = (f32[3,4,128]{2,1,0:T(4,128)S(1)}, f32[3,4,128]{2,1,0:T(4,128)S(1)}, u32[]{:S(2)}, u32[]{:S(2)}) collective-permute-start(f32[3,4,128]{2,1,0:T(4,128)S(1)} %multiply_add_fusion.1), channel_id=1, source_target_pairs={{0,32},{32,64},{64,96},{96,128},{128,160},{160,192},{192,224},{224... | collective-permute-start | bytes 18440 | tf_op jit(solution)/shard_map/ppermute | solution.py:20
  197.3 10.0 %collective-permute-start.2 = (f32[3,12,4]{2,1,0:T(8,128)S(1)}, f32[3,12,4]{2,1,0:T(8,128)S(1)}, u32[]{:S(2)}, u32[]{:S(2)}) collective-permute-start(f32[3,12,4]{2,1,0:T(8,128)S(1)} %get-tuple-element.66), channel_id=1, source_target_pairs={{0,1},{1,2},{2,3},{3,4},{4,5},{5,6},{6,7},{7,8},{8,9},{9,10},{10,1... | collective-permute-start | bytes 1736 | tf_op jit(solution)/shard_map/ppermute | solution.py:20
  200.4 6.9 %collective-permute-start.3 = (f32[3,12,4]{2,1,0:T(8,128)S(1)}, f32[3,12,4]{2,1,0:T(8,128)S(1)}, u32[]{:S(2)}, u32[]{:S(2)}) collective-permute-start(f32[3,12,4]{2,1,0:T(8,128)S(1)} %get-tuple-element.67), channel_id=1, source_target_pairs={{1,0},{2,1},{3,2},{4,3},{5,4},{6,5},{7,6},{8,7},{9,8},{10,9},{11,1... | collective-permute-start | bytes 1736 | tf_op jit(solution)/shard_map/ppermute | solution.py:23
  208.2 13.8 %copy-start.20 = (f32[1024]{0:T(1024)S(1)}, f32[1024]{0:T(1024)}, u32[]{:S(2)}) copy-start(f32[1024]{0:T(1024)} %param.21) | copy-start | bytes 12292
  208.2 13.8 %copy-start.21 = (f32[1024]{0:T(1024)S(1)}, f32[1024]{0:T(1024)}, u32[]{:S(2)}) copy-start(f32[1024]{0:T(1024)} %param.20) | copy-start | bytes 12292
  208.2 13.8 %copy-start.22 = (s32[1024]{0:T(1024)S(1)}, s32[1024]{0:T(1024)}, u32[]{:S(2)}) copy-start(s32[1024]{0:T(1024)} %param.19) | copy-start | bytes 12292
  237.3 2.6 collective-permute-start.5
  237.4 8.6 %collective-permute-start.4 = (f32[4,4,128]{2,1,0:T(4,128)S(1)}, f32[4,4,128]{2,1,0:T(4,128)S(1)}, u32[]{:S(2)}, u32[]{:S(2)}) collective-permute-start(f32[4,4,128]{2,1,0:T(4,128)S(1)} %pad_maximum_fusion.38), channel_id=1, source_target_pairs={{0,32},{32,64},{64,96},{96,128},{128,160},{160,192},{192,224},{224... | collective-permute-start | bytes 24584 | tf_op jit(solution)/shard_map/ppermute | solution.py:20
  246.1 14.3 %collective-permute-start.6 = (f32[4,12,4]{2,1,0:T(8,128)S(1)}, f32[4,12,4]{2,1,0:T(8,128)S(1)}, u32[]{:S(2)}, u32[]{:S(2)}) collective-permute-start(f32[4,12,4]{2,1,0:T(8,128)S(1)} %get-tuple-element.48), channel_id=1, source_target_pairs={{0,1},{1,2},{2,3},{3,4},{4,5},{5,6},{6,7},{7,8},{8,9},{9,10},{10,1... | collective-permute-start | bytes 2312 | tf_op jit(solution)/shard_map/ppermute | solution.py:20
  249.0 11.4 %collective-permute-start.7 = (f32[4,12,4]{2,1,0:T(8,128)S(1)}, f32[4,12,4]{2,1,0:T(8,128)S(1)}, u32[]{:S(2)}, u32[]{:S(2)}) collective-permute-start(f32[4,12,4]{2,1,0:T(8,128)S(1)} %get-tuple-element.49), channel_id=1, source_target_pairs={{1,0},{2,1},{3,2},{4,3},{5,4},{6,5},{7,6},{8,7},{9,8},{10,9},{11,1... | collective-permute-start | bytes 2312 | tf_op jit(solution)/shard_map/ppermute | solution.py:23
  298.2 7.0 %copy-start.9 = (f32[4096,256]{1,0:T(8,128)S(1)}, f32[4096,256]{1,0:T(8,128)}, u32[]{:S(2)}) copy-start(f32[4096,256]{1,0:T(8,128)} %get-tuple-element.94) | copy-start | bytes 12582916
  298.2 7.0 %copy-start.11 = (f32[4096,256]{1,0:T(8,128)S(1)}, f32[4096,256]{1,0:T(8,128)}, u32[]{:S(2)}) copy-start(f32[4096,256]{1,0:T(8,128)} %get-tuple-element.95) | copy-start | bytes 12582916
  332.0 7.0 %copy-start.5 = (f32[4096,256]{1,0:T(8,128)S(1)}, f32[4096,256]{1,0:T(8,128)}, u32[]{:S(2)}) copy-start(f32[4096,256]{1,0:T(8,128)} %get-tuple-element.92) | copy-start | bytes 12582916
  332.0 7.0 %copy-start.7 = (f32[4096,256]{1,0:T(8,128)S(1)}, f32[4096,256]{1,0:T(8,128)}, u32[]{:S(2)}) copy-start(f32[4096,256]{1,0:T(8,128)} %get-tuple-element.93) | copy-start | bytes 12582916
  339.0 22.4 %copy-start.17 = (f32[10,32,128]{2,1,0:T(8,128)S(1)}, f32[10,32,128]{2,1,0:T(8,128)}, u32[]{:S(2)}) copy-start(f32[10,32,128]{2,1,0:T(8,128)} %param.13) | copy-start | bytes 491524
  (4 other events, 16.4 us)
